TPU v7x, 512 devices: a whole 4x8x8 slice. The times are simulated.
512 devices in a mesh: dp: 16 (over z, core), mp: 32 (over y, x).
Axes of the slice: x: 4, y: 8, z: 8, core: 2. Of those that a mesh axis runs over, the one named last changes fastest.
Arguments:
- policy_hidden: bfloat16 [1024, 3584], P('dp'), may hold values from -96 to 96
- reference_hidden: bfloat16 [1024, 3584], P('dp'), may hold values from -96 to 96
- policy_gain: float32 [3584], replicated, may hold values from 0.5 to 1.5
- reference_gain: float32 [3584], replicated, may hold values from 0.5 to 1.5
- policy_embedding: bfloat16 [131072, 3584], P(('dp', 'mp')), may hold values from -1 to 1
- reference_embedding: bfloat16 [131072, 3584], P(('dp', 'mp')), may hold values from -1 to 1
- mixture_weight: float32 [1024], replicated, may hold values from 0.1 to 0.9
- sampled_tokens: int32 [1024], replicated, may hold values from 0 to 131071
Outputs:
- mixture_shift: float32 [1024, 131072], P(None, ('dp', 'mp'))
- sampled_logprobs: float32 [3, 1024], P(None, 'dp')
All inputs are finite; a program needn't handle non-finite values.
Results may differ from a plain program's by a relative error of at most 0.002.
Values may be sent and summed in bfloat16 or wider, within the bound.
No kernel may reach another device: no remote copies, remote signals or barrier semaphores. Data moves between devices by JAX's collectives and lax.ppermute only.
A program may use at most 64 MiB of HBM per device.

v0:
```python
import jax
import jax.numpy as jnp
from jax import lax
from jax.sharding import Mesh
from jax.sharding import PartitionSpec as P

DP = ("dp_0", "dp_1")
MP = ("mp_0", "mp_1")
DP_MP = ("dp_0", "dp_1", "mp_0", "mp_1")
softcap = 30.0
epsilon = 1e-06


def by_axis(x, axes):
    for axis in axes:
        x = lax.psum(x, axis)
    return x


def normalize(hidden, gain):
    values = hidden.astype(jnp.float32)
    meansq = jnp.mean(values * values, axis=-1, keepdims=True)
    return (values * lax.rsqrt(meansq + epsilon) * gain).astype(jnp.bfloat16)


def contract(normed, embedding):
    return lax.dot_general(
        normed, embedding, (((1,), (1,)), ((), ())), preferred_element_type=jnp.float32
    )


def local(
    policy_hidden,
    reference_hidden,
    policy_gain,
    reference_gain,
    policy_embedding,
    reference_embedding,
    mixture_weight,
    sampled_tokens,
):
    seq_local = policy_hidden.shape[0]
    vocab_local = policy_embedding.shape[0]
    stacked = jnp.stack(
        [normalize(policy_hidden, policy_gain), normalize(reference_hidden, reference_gain)]
    )
    piece = lax.all_gather(stacked, DP, axis=1, tiled=True)
    raw = jnp.stack([contract(piece[0], policy_embedding), contract(piece[1], reference_embedding)])
    capped = softcap * jnp.tanh(raw / softcap)
    capped_policy = capped[0]
    capped_reference = capped[1]
    weight = mixture_weight[:, None]
    mixed = (1.0 - weight) * capped_policy + weight * capped_reference
    shard = lax.axis_index(DP) * lax.axis_size(MP) + lax.axis_index(MP)
    first = shard * vocab_local
    columns = lax.broadcasted_iota(jnp.int32, (1, vocab_local), 1)
    onehot = (sampled_tokens[:, None] - first == columns).astype(jnp.float32)
    terms = (
        jnp.sum(jnp.exp(capped_policy), axis=1),
        jnp.sum(jnp.exp(capped_reference), axis=1),
        jnp.sum(jnp.exp(mixed), axis=1),
        jnp.sum(onehot * capped_policy, axis=1),
        jnp.sum(onehot * capped_reference, axis=1),
    )
    policy_sum, reference_sum, mixture_sum, policy_pick, reference_pick = (
        by_axis(terms[0], DP_MP),
        by_axis(terms[1], DP_MP),
        by_axis(terms[2], DP_MP),
        by_axis(terms[3], DP_MP),
        by_axis(terms[4], DP_MP),
    )
    policy_total = jnp.log(policy_sum)
    reference_total = jnp.log(reference_sum)
    mixture_total = jnp.log(mixture_sum)
    mixed_pick = (1.0 - mixture_weight) * policy_pick + mixture_weight * reference_pick
    policy_logp = policy_pick - policy_total
    reference_logp = reference_pick - reference_total
    mixture_logp = mixed_pick - mixture_total
    mixture_shift = mixed - mixture_total[:, None] - (capped_policy - policy_total[:, None])
    every_logp = jnp.stack([policy_logp, reference_logp, mixture_logp])
    sampled_logprobs = lax.dynamic_slice_in_dim(
        every_logp, lax.axis_index(DP) * seq_local, seq_local, 1
    )
    return (mixture_shift, sampled_logprobs)


def solution(mesh):
    split = Mesh(mesh.devices.reshape(8, 2, 8, 4), ("dp_0", "dp_1", "mp_0", "mp_1"))
    in_specs = (P(DP, None), P(DP, None), P(), P(), P(DP_MP, None), P(DP_MP, None), P(), P())
    out_specs = (P(None, DP_MP), P(None, DP))
    return jax.shard_map(local, mesh=split, in_specs=in_specs, out_specs=out_specs, check_vma=False)
```

profile of v0, /device:TPU:4, one launch (start us, length us, event | category | flops | bytes accessed | tf_op | source)
XLA Modules:
  0.0 205.5 jit_solution(13288046181011595460)
XLA Ops:
  7.2 0.0 copy-start
  7.2 0.0 all-gather.2.cloned.1.call-start
  7.2 1.3 fusion.9
  8.6 1.2 fusion.6
  9.8 0.0 copy-start.2
  9.8 0.0 copy-start.3
  9.8 1.5 fusion.12
  11.3 1.0 pad_maximum_fusion
  12.3 0.0 all-gather.2.cloned.1.call-update
  12.4 93.7 %all-gather.2.cloned.1.call-done = bf16[2,1024,3584]{2,1,0:T(8,128)(2,1)} async-done(((bf16[2,64,3584]{2,1,0:T(8,128)(2,1)}), bf16[2,1024,3584]{2,1,0:T(8,128)(2,1)}) %all-gather.2.cloned.1.call-update) | async-done | bytes 14680080 | tf_op jit(solution)/shard_map/all_gather | solution.py:47
  106.1 5.3 %fusion.5 = f32[1,1024,256]{1,2,0:T(8,128)S(1)} fusion(bf16[256,3584]{1,0:T(8,128)(2,1)S(1)} %copy-done, bf16[2,1024,3584]{2,1,0:T(8,128)(2,1)} %all-gather.2.cloned.1.call-done), kind=kOutput, calls=%fused_computation.8 | convolution fusion | flops 1879048192 | bytes 10223616 | tf_op jit(solution)/shard_map/dot_general | solution.py:27
  111.4 1.9 copy-done.4
  113.3 0.5 copy-done.5
  113.9 2.1 %fusion.4 = f32[1,1024,256]{1,2,0:T(8,128)S(1)} fusion(bf16[256,3584]{1,0:T(8,128)(2,1)S(1)} %copy-done.5, bf16[2,1024,3584]{2,1,0:T(8,128)(2,1)S(1)} %copy-done.4), kind=kOutput, calls=%fused_computation.7 | convolution fusion | flops 1879048192 | bytes 10223616 | tf_op jit(solution)/shard_map/dot_general | solution.py:27
  115.9 0.3 fusion.3
  116.2 1.3 copy-done.1
  117.6 0.6 select_reduce_fusion
  118.2 28.2 %all-reduce.1 = (f32[1024]{0:T(1024)S(1)}, f32[1024]{0:T(1024)S(1)}, f32[1024]{0:T(1024)S(1)}, f32[1024]{0:T(1024)S(1)}, f32[1024]{0:T(1024)S(1)}) all-reduce(f32[1024]{0:T(1024)S(1)} %get-tuple-element.8, f32[1024]{0:T(1024)S(1)} %get-tuple-element.7, ...), channel_id=1, replica_groups=mesh['dp_0'=8,'dp_1'=2,'mp_0'=8,'mp_1'=4] {'dp_0'}, use_global_device_ids=true, to_apply=%region_8.0 | all-reduce | flops 5120 | bytes 40960 | tf_op jit(solution)/shard_map/psum | solution.py:16
  146.4 3.4 %all-reduce.3 = (f32[1024]{0:T(1024)S(1)}, f32[1024]{0:T(1024)S(1)}, f32[1024]{0:T(1024)S(1)}, f32[1024]{0:T(1024)S(1)}, f32[1024]{0:T(1024)S(1)}) all-reduce(f32[1024]{0:T(1024)S(1)} %get-tuple-element.14, f32[1024]{0:T(1024)S(1)} %get-tuple-element.15, ...), channel_id=1, replica_groups=mesh['dp_0'=8,'dp_1'=2,'mp_0'=8,'mp_1'=4] {'dp_1'}, use_global_device_ids=true, to_apply=%region_9.0 | all-reduce | flops 5120 | bytes 40960 | tf_op jit(solution)/shard_map/psum | solution.py:16
  149.8 29.7 %all-reduce = (f32[1024]{0:T(1024)S(1)}, f32[1024]{0:T(1024)S(1)}, f32[1024]{0:T(1024)S(1)}, f32[1024]{0:T(1024)S(1)}, f32[1024]{0:T(1024)S(1)}) all-reduce(f32[1024]{0:T(1024)S(1)} %get-tuple-element.24, f32[1024]{0:T(1024)S(1)} %get-tuple-element.25, ...), channel_id=1, replica_groups=mesh['dp_0'=8,'dp_1'=2,'mp_0'=8,'mp_1'=4] {'mp_0'}, use_global_device_ids=true, to_apply=%region_10.0 | all-reduce | flops 5120 | bytes 40960 | tf_op jit(solution)/shard_map/psum | solution.py:16
  179.5 15.4 %all-reduce.2 = (f32[1024]{0:T(1024)S(1)}, f32[1024]{0:T(1024)S(1)}, f32[1024]{0:T(1024)S(1)}, f32[1024]{0:T(1024)S(1)}, f32[1024]{0:T(1024)S(1)}) all-reduce(f32[1024]{0:T(1024)S(1)} %get-tuple-element.9, f32[1024]{0:T(1024)S(1)} %get-tuple-element.10, ...), channel_id=1, replica_groups=mesh['dp_0'=8,'dp_1'=2,'mp_0'=8,'mp_1'=4] {'mp_1'}, use_global_device_ids=true, to_apply=%region_11.0 | all-reduce | flops 5120 | bytes 40960 | tf_op jit(solution)/shard_map/psum | solution.py:16
  194.9 1.8 subtract_subtract_fusion
  196.7 1.3 copy.10
  198.0 0.7 fusion.15
  (11 shorter events, 0.0 us)
Async XLA Ops:
  7.2 98.9 %copy-start = (bf16[256,3584]{1,0:T(8,128)(2,1)S(1)}, bf16[256,3584]{1,0:T(8,128)(2,1)}, u32[]{:S(2)}) copy-start(bf16[256,3584]{1,0:T(8,128)(2,1)} %param.13) | copy-start | bytes 5505028
  7.2 98.9 %all-gather.2.cloned.1.call-start = ((), (), s32[]{:S(2)}) async-start(), calls=%async_computation | async-start | bytes 15597568 | tf_op jit(solution)/shard_map/all_gather | solution.py:47
  9.8 2.6 %copy-start.2 = (f32[1024]{0:T(1024)S(1)}, f32[1024]{0:T(1024)}, u32[]{:S(2)}) copy-start(f32[1024]{0:T(1024)} %param.14) | copy-start | bytes 12292
  9.8 2.6 %copy-start.3 = (s32[1024]{0:T(1024)S(1)}, s32[1024]{0:T(1024)}, u32[]{:S(2)}) copy-start(s32[1024]{0:T(1024)} %param.15) | copy-start | bytes 12292
  106.1 7.3 %copy-start.4 = (bf16[2,1024,3584]{2,1,0:T(8,128)(2,1)S(1)}, bf16[2,1024,3584]{2,1,0:T(8,128)(2,1)}, u32[]{:S(2)}) copy-start(bf16[2,1024,3584]{2,1,0:T(8,128)(2,1)} %all-gather.2.cloned.1.call-done) | copy-start | bytes 44040196
  106.1 7.8 %copy-start.5 = (bf16[256,3584]{1,0:T(8,128)(2,1)S(1)}, bf16[256,3584]{1,0:T(8,128)(2,1)}, u32[]{:S(2)}) copy-start(bf16[256,3584]{1,0:T(8,128)(2,1)} %param.12) | copy-start | bytes 5505028
  116.2 1.4 copy-start.1
Sparse Core Ops, SparseCore 0:
  12.5 93.5 all-gather.1
where the time goes:
time: 206 us
  waiting for transfers between devices  93.7 us (45%)
  blocking collectives  76.7 us (37%)
  between operations  14.2 us (7%)
  other arithmetic  8.41 us (4%)
  matrix products  7.39 us (4%)
  local copies, waits for them, and re-layouts  5.12 us (2%)
    all_gather x1, waiting for transfers between devices, local(): piece = lax.all_gather(stacked, DP, axis=1, tiled=True)  93.7 us
    psum x4, blocking collectives, by_axis(): x = lax.psum(x, axis)  76.7 us
    dot_general x2, matrix products, contract(): lax.dot_general(normed, embedding, (((1,), (1,)), ((), ())), preferred_el...  7.39 us
    unnamed x13, local copies, waits for them, and re-layouts  5.12 us
  transfers between devices with their start and end apart: 1, of which 1 were waited for; matrix products, arithmetic and copies ran while one was open for 0% of the time, Pallas kernels for 0%

commit v1 on v0

--- a/solution.py
+++ b/solution.py
@@ -13,7 +13,11 @@
 
 def by_axis(x, axes):
     for axis in axes:
-        x = lax.psum(x, axis)
+
+        def map_local_data(v0):
+            return lax.all_gather(v0, axis_name=axis).sum(axis=0)
+
+        x = map_local_data(x)
     return x
 
 

time: 206 us -> 444 us (2.16)
  the two profiles are of different devices: /device:TPU:4 before, /device:TPU:16 now
where the time goes in v1:
time: 444 us
  blocking collectives  315 us (71%)
  waiting for transfers between devices  93.6 us (21%)
  between operations  14.3 us (3%)
  other arithmetic  8.74 us (2%)
  matrix products  7.39 us (2%)
  local copies, waits for them, and re-layouts  5.36 us (1%)
    all_gather x20, blocking collectives, map_local_data(): return lax.all_gather(v0, axis_name=axis).sum(axis=0)  315 us
    all_gather x1, waiting for transfers between devices, local(): piece = lax.all_gather(stacked, DP, axis=1, tiled=True)  93.5 us
  transfers between devices with their start and end apart: 1, of which 1 were waited for; matrix products, arithmetic and copies ran while one was open for 0% of the time, Pallas kernels for 0%

profile of v1, /device:TPU:16, one launch (start us, length us, event | category | flops | bytes accessed | tf_op | source)
XLA Modules:
  0.0 443.9 jit_solution(18201611409883514248)
XLA Ops:
  12.4 93.5 %all-gather.22.cloned.1.call-done = bf16[2,1024,3584]{2,1,0:T(8,128)(2,1)} async-done(((bf16[2,64,3584]{2,1,0:T(8,128)(2,1)}), bf16[2,1024,3584]{2,1,0:T(8,128)(2,1)}) %all-gather.22.cloned.1.call-update) | async-done | bytes 14680080 | tf_op jit(solution)/shard_map/all_gather | solution.py:51
  106.0 5.3 %fusion.5 = f32[1,1024,256]{1,2,0:T(8,128)S(1)} fusion(bf16[256,3584]{1,0:T(8,128)(2,1)S(1)} %copy-done, bf16[2,1024,3584]{2,1,0:T(8,128)(2,1)} %all-gather.22.cloned.1.call-done), kind=kOutput, calls=%fused_computation.8 | convolution fusion | flops 1879048192 | bytes 10223616 | tf_op jit(solution)/shard_map/dot_general | solution.py:31
  111.3 1.9 copy-done.4
  113.7 2.1 fusion.4
  118.1 24.5 %all-gather.12 = f32[8192]{0:T(1024)S(1)} all-gather(f32[1024]{0:T(1024)S(1)} %get-tuple-element.8), channel_id=14, replica_groups=mesh['dp_0'=8,'dp_1'=2,'mp_0'=8,'mp_1'=4] {'dp_0'}, dimensions={0}, use_global_device_ids=true | all-gather | bytes 36864 | tf_op jit(solution)/shard_map/all_gather | solution.py:18
  142.6 1.8 all-gather.13
  144.4 25.4 %all-gather.14 = f32[8192]{0:T(1024)S(1)} all-gather(f32[1024]{0:T(1024)S(1)} %reduce_sum.262), channel_id=16, replica_groups=mesh['dp_0'=8,'dp_1'=2,'mp_0'=8,'mp_1'=4] {'mp_0'}, dimensions={0}, use_global_device_ids=true | all-gather | bytes 36864 | tf_op jit(solution)/shard_map/all_gather | solution.py:18
  169.8 12.2 %all-gather.15 = f32[4096]{0:T(1024)S(1)} all-gather(f32[1024]{0:T(1024)S(1)} %reduce_sum.263), channel_id=17, replica_groups=mesh['dp_0'=8,'dp_1'=2,'mp_0'=8,'mp_1'=4] {'mp_1'}, dimensions={0}, use_global_device_ids=true | all-gather | bytes 20480 | tf_op jit(solution)/shard_map/all_gather | solution.py:18
  182.1 24.5 %all-gather.8 = f32[8192]{0:T(1024)S(1)} all-gather(f32[1024]{0:T(1024)S(1)} %get-tuple-element.9), channel_id=10, replica_groups=mesh['dp_0'=8,'dp_1'=2,'mp_0'=8,'mp_1'=4] {'dp_0'}, dimensions={0}, use_global_device_ids=true | all-gather | bytes 36864 | tf_op jit(solution)/shard_map/all_gather | solution.py:18
  206.6 1.8 all-gather.9
  208.4 24.5 %all-gather.10 = f32[8192]{0:T(1024)S(1)} all-gather(f32[1024]{0:T(1024)S(1)} %reduce_sum.257), channel_id=12, replica_groups=mesh['dp_0'=8,'dp_1'=2,'mp_0'=8,'mp_1'=4] {'mp_0'}, dimensions={0}, use_global_device_ids=true | all-gather | bytes 36864 | tf_op jit(solution)/shard_map/all_gather | solution.py:18
  232.9 11.9 %all-gather.11 = f32[4096]{0:T(1024)S(1)} all-gather(f32[1024]{0:T(1024)S(1)} %reduce_sum.258), channel_id=13, replica_groups=mesh['dp_0'=8,'dp_1'=2,'mp_0'=8,'mp_1'=4] {'mp_1'}, dimensions={0}, use_global_device_ids=true | all-gather | bytes 20480 | tf_op jit(solution)/shard_map/all_gather | solution.py:18
  244.9 24.5 %all-gather = f32[8192]{0:T(1024)S(1)} all-gather(f32[1024]{0:T(1024)S(1)} %get-tuple-element.11), channel_id=2, replica_groups=mesh['dp_0'=8,'dp_1'=2,'mp_0'=8,'mp_1'=4] {'dp_0'}, dimensions={0}, use_global_device_ids=true | all-gather | bytes 36864 | tf_op jit(solution)/shard_map/all_gather | solution.py:18
  269.4 1.8 all-gather.1
  271.2 24.5 %all-gather.2 = f32[8192]{0:T(1024)S(1)} all-gather(f32[1024]{0:T(1024)S(1)} %reduce_sum.247), channel_id=4, replica_groups=mesh['dp_0'=8,'dp_1'=2,'mp_0'=8,'mp_1'=4] {'mp_0'}, dimensions={0}, use_global_device_ids=true | all-gather | bytes 36864 | tf_op jit(solution)/shard_map/all_gather | solution.py:18
  295.7 11.9 %all-gather.3 = f32[4096]{0:T(1024)S(1)} all-gather(f32[1024]{0:T(1024)S(1)} %reduce_sum.248), channel_id=5, replica_groups=mesh['dp_0'=8,'dp_1'=2,'mp_0'=8,'mp_1'=4] {'mp_1'}, dimensions={0}, use_global_device_ids=true | all-gather | bytes 20480 | tf_op jit(solution)/shard_map/all_gather | solution.py:18
  307.7 24.5 %all-gather.4 = f32[8192]{0:T(1024)S(1)} all-gather(f32[1024]{0:T(1024)S(1)} %get-tuple-element.12), channel_id=6, replica_groups=mesh['dp_0'=8,'dp_1'=2,'mp_0'=8,'mp_1'=4] {'dp_0'}, dimensions={0}, use_global_device_ids=true | all-gather | bytes 36864 | tf_op jit(solution)/shard_map/all_gather | solution.py:18
  332.2 1.8 all-gather.5
  334.0 24.5 %all-gather.6 = f32[8192]{0:T(1024)S(1)} all-gather(f32[1024]{0:T(1024)S(1)} %reduce_sum.252), channel_id=8, replica_groups=mesh['dp_0'=8,'dp_1'=2,'mp_0'=8,'mp_1'=4] {'mp_0'}, dimensions={0}, use_global_device_ids=true | all-gather | bytes 36864 | tf_op jit(solution)/shard_map/all_gather | solution.py:18
  358.5 11.9 %all-gather.7 = f32[4096]{0:T(1024)S(1)} all-gather(f32[1024]{0:T(1024)S(1)} %reduce_sum.253), channel_id=9, replica_groups=mesh['dp_0'=8,'dp_1'=2,'mp_0'=8,'mp_1'=4] {'mp_1'}, dimensions={0}, use_global_device_ids=true | all-gather | bytes 20480 | tf_op jit(solution)/shard_map/all_gather | solution.py:18
  370.5 24.5 %all-gather.16 = f32[8192]{0:T(1024)S(1)} all-gather(f32[1024]{0:T(1024)S(1)} %get-tuple-element.10), channel_id=18, replica_groups=mesh['dp_0'=8,'dp_1'=2,'mp_0'=8,'mp_1'=4] {'dp_0'}, dimensions={0}, use_global_device_ids=true | all-gather | bytes 36864 | tf_op jit(solution)/shard_map/all_gather | solution.py:18
  395.0 1.8 all-gather.17
  396.8 24.5 %all-gather.18 = f32[8192]{0:T(1024)S(1)} all-gather(f32[1024]{0:T(1024)S(1)} %reduce_sum.267), channel_id=20, replica_groups=mesh['dp_0'=8,'dp_1'=2,'mp_0'=8,'mp_1'=4] {'mp_0'}, dimensions={0}, use_global_device_ids=true | all-gather | bytes 36864 | tf_op jit(solution)/shard_map/all_gather | solution.py:18
  421.3 11.9 %all-gather.19 = f32[4096]{0:T(1024)S(1)} all-gather(f32[1024]{0:T(1024)S(1)} %reduce_sum.268), channel_id=21, replica_groups=mesh['dp_0'=8,'dp_1'=2,'mp_0'=8,'mp_1'=4] {'mp_1'}, dimensions={0}, use_global_device_ids=true | all-gather | bytes 20480 | tf_op jit(solution)/shard_map/all_gather | solution.py:18
  (67 shorter events, 12.2 us)
Async XLA Ops:
  7.2 98.8 %copy-start = (bf16[256,3584]{1,0:T(8,128)(2,1)S(1)}, bf16[256,3584]{1,0:T(8,128)(2,1)}, u32[]{:S(2)}) copy-start(bf16[256,3584]{1,0:T(8,128)(2,1)} %param.13) | copy-start | bytes 5505028
  7.2 98.8 %all-gather.22.cloned.1.call-start = ((), (), s32[]{:S(2)}) async-start(), calls=%async_computation | async-start | bytes 15597568 | tf_op jit(solution)/shard_map/all_gather | solution.py:51
  9.8 2.6 copy-start.2
  9.8 2.6 copy-start.3
  105.9 7.3 %copy-start.4 = (bf16[2,1024,3584]{2,1,0:T(8,128)(2,1)S(1)}, bf16[2,1024,3584]{2,1,0:T(8,128)(2,1)}, u32[]{:S(2)}) copy-start(bf16[2,1024,3584]{2,1,0:T(8,128)(2,1)} %all-gather.22.cloned.1.call-done) | copy-start | bytes 44040196
  106.0 7.8 %copy-start.5 = (bf16[256,3584]{1,0:T(8,128)(2,1)S(1)}, bf16[256,3584]{1,0:T(8,128)(2,1)}, u32[]{:S(2)}) copy-start(bf16[256,3584]{1,0:T(8,128)(2,1)} %param.12) | copy-start | bytes 5505028
  116.1 1.4 copy-start.1
Sparse Core Ops, SparseCore 0:
  12.5 93.4 all-gather.21

commit v2 on v0

--- a/solution.py
+++ b/solution.py
@@ -44,7 +44,8 @@
     stacked = jnp.stack(
         [normalize(policy_hidden, policy_gain), normalize(reference_hidden, reference_gain)]
     )
-    piece = lax.all_gather(stacked, DP, axis=1, tiled=True)
+    sent = jnp.stack([stacked] * lax.axis_size(DP))
+    piece = jnp.concatenate(lax.all_to_all(sent, DP, 0, 0), axis=1)
     raw = jnp.stack([contract(piece[0], policy_embedding), contract(piece[1], reference_embedding)])
     capped = softcap * jnp.tanh(raw / softcap)
     capped_policy = capped[0]

time: 206 us -> 436 us (2.12)
  waiting for transfers between devices: 93.7 us -> 319 us
  between operations: 14.2 us -> 0.8 us
  local copies, waits for them, and re-layouts: 5.12 us -> 15.7 us
  starting transfers between devices: 0.04 us -> 10.6 us
    all_to_all x0 -> x1, waiting for transfers between devices: none -> 319 us  [local(): piece = jnp.concatenate(lax.all_to_all(sent, DP, 0, 0), axis=1)]
    all_gather x1 -> x0, waiting for transfers between devices: 93.7 us -> none  [local(): piece = lax.all_gather(stacked, DP, axis=1, tiled=True)]
    all_to_all x0 -> x1, starting transfers between devices: none -> 10.6 us  [local(): piece = jnp.concatenate(lax.all_to_all(sent, DP, 0, 0), axis=1)]
    another operation x0 -> x1, local copies, waits for them, and re-layouts: none -> 6.89 us  [local(): sent = jnp.stack([stacked] * lax.axis_size(DP))]
    slice x0 -> x1, local copies, waits for them, and re-layouts: none -> 6.18 us  [local(): piece[0]]
where the time goes in v2:
time: 436 us
  waiting for transfers between devices  319 us (73%)
  blocking collectives  77.9 us (18%)
  local copies, waits for them, and re-layouts  15.7 us (4%)
  starting transfers between devices  10.6 us (2%)
  other arithmetic  7.49 us (2%)
    all_to_all x1, waiting for transfers between devices, local(): piece = jnp.concatenate(lax.all_to_all(sent, DP, 0, 0), axis=1)  319 us
    psum x4, blocking collectives, by_axis(): x = lax.psum(x, axis)  77.9 us
    all_to_all x1, starting transfers between devices, local(): piece = jnp.concatenate(lax.all_to_all(sent, DP, 0, 0), axis=1)  10.6 us
  transfers between devices with their start and end apart: 1, of which 1 were waited for; matrix products, arithmetic and copies ran while one was open for 0% of the time, Pallas kernels for 0%

profile of v2, /device:TPU:4, one launch (start us, length us, event | category | flops | bytes accessed | tf_op | source)
XLA Modules:
  0.0 435.6 jit_solution(17446743777192592667)
XLA Ops:
  0.6 0.0 copy-start
  0.6 1.3 fusion.5
  2.0 1.2 fusion.2
  3.2 1.5 fusion.8
  4.7 0.1 pad_maximum_fusion
  4.8 6.9 %stack.25 = bf16[16,2,64,3584]{3,2,1,0:T(8,128)(2,1)} broadcast(bf16[2,64,3584]{2,1,0:T(8,128)(2,1)S(1)} %pad_maximum_fusion), dimensions={1,2,3} | broadcast | bytes 15597568 | tf_op jit(solution)/shard_map/stack | solution.py:47
  11.7 10.6 %all-to-all-start = ((bf16[16,2,64,3584]{3,2,1,0:T(8,128)(2,1)}), bf16[16,2,64,3584]{3,2,1,0:T(8,128)(2,1)}, u32[]{:S(2)}, u32[]{:S(2)}) async-start(bf16[16,2,64,3584]{3,2,1,0:T(8,128)(2,1)} %stack.25), calls=%async_computation | async-start | bytes 29360128 | tf_op jit(solution)/shard_map/all_to_all | solution.py:48
  22.3 0.0 copy-done.2
  22.3 0.0 copy-done.3
  22.4 318.9 %all-to-all-done = bf16[16,2,64,3584]{3,2,1,0:T(8,128)(2,1)} async-done(((bf16[16,2,64,3584]{3,2,1,0:T(8,128)(2,1)}), bf16[16,2,64,3584]{3,2,1,0:T(8,128)(2,1)}, u32[]{:S(2)}, u32[]{:S(2)}) %all-to-all-start) | async-done | bytes 14680096 | tf_op jit(solution)/shard_map/all_to_all | solution.py:48
  341.3 6.2 %fusion.12 = (bf16[1,16,64,3584]{3,2,0,1:T(8,128)(2,1)S(1)}, bf16[1,16,64,3584]{3,2,0,1:T(8,128)(2,1)S(1)}) fusion(bf16[2,16,64,3584]{3,2,0,1:T(8,128)(2,1)} %bitcast.2), kind=kLoop, calls=%fused_computation.40 | loop fusion | bytes 29360128 | tf_op jit(solution)/shard_map/slice | solution.py:49
  347.5 0.0 copy-start.4
  347.5 2.1 convolution_bitcast_fusion
  349.6 2.1 convolution_bitcast_fusion.1
  351.7 0.3 fusion.1
  352.0 1.3 copy-done.1
  353.3 0.6 select_reduce_fusion
  354.0 28.7 %all-reduce.1 = (f32[1024]{0:T(1024)S(1)}, f32[1024]{0:T(1024)S(1)}, f32[1024]{0:T(1024)S(1)}, f32[1024]{0:T(1024)S(1)}, f32[1024]{0:T(1024)S(1)}) all-reduce(f32[1024]{0:T(1024)S(1)} %get-tuple-element.8, f32[1024]{0:T(1024)S(1)} %get-tuple-element.7, ...), channel_id=1, replica_groups=mesh['dp_0'=8,'dp_1'=2,'mp_0'=8,'mp_1'=4] {'dp_0'}, use_global_device_ids=true, to_apply=%region_8.0 | all-reduce | flops 5120 | bytes 40960 | tf_op jit(solution)/shard_map/psum | solution.py:16
  382.7 3.4 all-reduce.3
  386.1 30.4 %all-reduce = (f32[1024]{0:T(1024)S(1)}, f32[1024]{0:T(1024)S(1)}, f32[1024]{0:T(1024)S(1)}, f32[1024]{0:T(1024)S(1)}, f32[1024]{0:T(1024)S(1)}) all-reduce(f32[1024]{0:T(1024)S(1)} %get-tuple-element.24, f32[1024]{0:T(1024)S(1)} %get-tuple-element.25, ...), channel_id=1, replica_groups=mesh['dp_0'=8,'dp_1'=2,'mp_0'=8,'mp_1'=4] {'mp_0'}, use_global_device_ids=true, to_apply=%region_10.0 | all-reduce | flops 5120 | bytes 40960 | tf_op jit(solution)/shard_map/psum | solution.py:16
  416.5 15.4 %all-reduce.2 = (f32[1024]{0:T(1024)S(1)}, f32[1024]{0:T(1024)S(1)}, f32[1024]{0:T(1024)S(1)}, f32[1024]{0:T(1024)S(1)}, f32[1024]{0:T(1024)S(1)}) all-reduce(f32[1024]{0:T(1024)S(1)} %get-tuple-element.9, f32[1024]{0:T(1024)S(1)} %get-tuple-element.10, ...), channel_id=1, replica_groups=mesh['dp_0'=8,'dp_1'=2,'mp_0'=8,'mp_1'=4] {'mp_1'}, use_global_device_ids=true, to_apply=%region_11.0 | all-reduce | flops 5120 | bytes 40960 | tf_op jit(solution)/shard_map/psum | solution.py:16
  431.9 1.8 subtract_subtract_fusion
  433.7 1.3 copy.10
  435.0 0.7 fusion.11
  (10 shorter events, 0.0 us)
Async XLA Ops:
  0.6 346.9 %copy-start = (bf16[256,3584]{1,0:T(8,128)(2,1)S(1)}, bf16[256,3584]{1,0:T(8,128)(2,1)}, u32[]{:S(2)}) copy-start(bf16[256,3584]{1,0:T(8,128)(2,1)} %param.13) | copy-start | bytes 5505028
  11.7 10.6 %copy-start.2 = (f32[1024]{0:T(1024)S(1)}, f32[1024]{0:T(1024)}, u32[]{:S(2)}) copy-start(f32[1024]{0:T(1024)} %param.14) | copy-start | bytes 12292
  11.7 10.6 %copy-start.3 = (s32[1024]{0:T(1024)S(1)}, s32[1024]{0:T(1024)}, u32[]{:S(2)}) copy-start(s32[1024]{0:T(1024)} %param.15) | copy-start | bytes 12292
  11.7 329.6 %all-to-all-start = ((bf16[16,2,64,3584]{3,2,1,0:T(8,128)(2,1)}), bf16[16,2,64,3584]{3,2,1,0:T(8,128)(2,1)}, u32[]{:S(2)}, u32[]{:S(2)}) async-start(bf16[16,2,64,3584]{3,2,1,0:T(8,128)(2,1)} %stack.25), calls=%async_computation | async-start | bytes 29360128 | tf_op jit(solution)/shard_map/all_to_all | solution.py:48
  347.5 2.1 copy-start.4
  352.0 1.4 copy-start.1
